TPU v7x, 512 devices: a whole 4x8x8 slice. The times are simulated.
512 devices in a mesh: lvl: 128 (over y, z_hi, x), col: 4 (over z_lo, core).
Axes of the slice: x: 4, y: 8, z: 8 (z_hi: 4, z_lo: 2; z = z_hi * 2 + z_lo), core: 2. Of those that a mesh axis runs over, the one named last changes fastest.
Arguments:
- up_blocks: float32 [256, 512, 512], P('lvl', None, 'col'), may hold values from -1.25 to 1.25
- level_blocks: float32 [256, 512, 512], P('lvl', None, 'col'), may hold values from -11 to 2, as said below
- down_blocks: float32 [256, 512, 512], P('lvl', None, 'col'), may hold values from -1.25 to 1.25
Outputs:
- reduced_level: float32 [128, 512, 512], P('lvl', None, 'col')
- reduced_up: float32 [128, 512, 512], P('lvl', None, 'col')
- reduced_down: float32 [128, 512, 512], P('lvl', None, 'col')
Inputs may be any that keep to these rules, and one draw needn't show every extreme that they name: `level_blocks`: every diagonal entry of every level's block is -1 or less.
All inputs are finite; a program needn't handle non-finite values.
Results may differ from a plain program's by a relative error of at most 0.00013.
Values sent between devices are 32-bit elements; how exact they have to be, the bound alone decides.
A program may use at most 64 MiB of HBM per device.

v0:
```python
import jax
import jax.numpy as jnp
from jax import lax
from jax.sharding import PartitionSpec as P

SWEEPS = 2


def from_behind(block, axis, distance):
    devices = range(lax.axis_size(axis))
    route = [(i - distance, i) for i in devices if i - distance in devices]
    return lax.ppermute(block, axis, route)


def per_device(up_blocks, level_blocks, down_blocks):
    col_share = level_blocks.shape[2]
    odd_level = level_blocks[1::2]
    right_side = jnp.concatenate([up_blocks[1::2], down_blocks[1::2]], axis=2)
    full_level, full_up, full_down = (
        lax.all_gather(odd_level, "col", axis=2, tiled=True),
        lax.all_gather(up_blocks[0::2], "col", axis=2, tiled=True),
        lax.all_gather(down_blocks[0::2], "col", axis=2, tiled=True),
    )
    out_rates = -jnp.diagonal(full_level, axis1=1, axis2=2)
    inverse = (1.0 / out_rates)[:, :, None]
    solution = right_side * inverse
    for sweep_no in range(SWEEPS):
        product = jnp.einsum(
            "lpk,lkc->lpc",
            full_level,
            solution,
            precision=lax.Precision.HIGHEST,
            preferred_element_type=jnp.float32,
        )
        solution = (right_side + product + out_rates[:, :, None] * solution) * inverse
    from_below = from_behind(solution[-1], "lvl", 1)
    lower_side = jnp.concatenate([from_below[None], solution[:-1]], axis=0)
    upper_terms = jnp.einsum(
        "lpk,lkc->lpc",
        full_up,
        solution,
        precision=lax.Precision.HIGHEST,
        preferred_element_type=jnp.float32,
    )
    lower_terms = jnp.einsum(
        "lpk,lkc->lpc",
        full_down,
        lower_side,
        precision=lax.Precision.HIGHEST,
        preferred_element_type=jnp.float32,
    )
    row_start = lax.axis_index("col") * col_share
    own_square = lax.dynamic_slice_in_dim(level_blocks, row_start, col_share, 1)
    local_peak = jnp.max(-jnp.diagonal(own_square, axis1=1, axis2=2))
    top_rate = lax.pmax(local_peak, ("lvl", "col"))
    reduced_level = (
        level_blocks[0::2] + upper_terms[:, :, col_share:] + lower_terms[:, :, :col_share]
    ) / top_rate
    reduced_up = upper_terms[:, :, :col_share] / top_rate
    reduced_down = lower_terms[:, :, col_share:] / top_rate
    return (reduced_level, reduced_up, reduced_down)


def solution(mesh):
    placed = (P("lvl", None, "col"), P("lvl", None, "col"), P("lvl", None, "col"))
    return jax.shard_map(
        per_device,
        mesh=mesh,
        in_specs=placed,
        out_specs=(P("lvl", None, "col"), P("lvl", None, "col"), P("lvl", None, "col")),
        check_vma=False,
    )
```

profile of v0, /device:TPU:57, one launch (start us, length us, event | category | flops | bytes accessed | tf_op | source)
XLA Modules:
  0.0 193.6 jit_solution(3153033945648968497)
XLA Ops:
  7.2 0.0 all-gather.4.cloned.1.call-start
  7.2 1.8 fusion.18
  9.0 0.0 all-gather.4.cloned.1.call-update
  9.0 0.0 all-gather.6.cloned.1.call-start
  9.1 1.8 fusion.17
  10.8 0.0 all-gather.6.cloned.1.call-update
  10.8 0.0 all-gather.8.cloned.1.call-start
  10.9 1.8 fusion.19
  12.7 0.0 all-gather.8.cloned.1.call-update
  12.7 0.1 copy.21
  12.8 0.1 copy.22
  13.0 28.2 %all-gather.4.cloned.1.call-done = f32[1,512,512]{2,1,0:T(8,128)} async-done(((f32[1,512,128]{2,1,0:T(8,128)}), f32[1,512,512]{2,1,0:T(8,128)}) %all-gather.4.cloned.1.call-update) | async-done | bytes 1048592 | tf_op jit(solution)/shard_map/all_gather | solution.py:20
  41.2 8.5 %gather_fusion = f32[512]{0:T(512)S(1)} fusion(f32[512,512]{1,0:T(8,128)} %bitcast.49, s32[512]{0:T(512)S(1)} %bitcast.48), kind=kCustom, calls=%fused_computation | custom fusion | bytes 8192 | tf_op jit(solution)/shard_map/jit(diagonal)/gather | solution.py:24
  49.7 2.3 %fusion.4 = f32[512,256]{0,1:T(8,128)S(1)} fusion(f32[1,512,1,1,1,1,128]{1,6,5,4,3,2,0:T(8,128)S(1)} %bitcast.53, f32[1,512,1,1,1,1,128]{1,6,5,4,3,2,0:T(8,128)S(1)} %bitcast.50, f32[512,128]{0,1:T(8,128)S(1)} %bitcast.54, f32[512,128]{0,1:T(8,128)S(1)} %bitcast.51, f32[512]{0:T(512)S(1)} %get-tuple-element.19, f32[512]{0:T(512)S(1)} %get-tuple-element.18, ...), kind=kOutput, calls=%fused_computation.10 | convolution fusion | flops 806354944 | bytes 2625536 | tf_op jit(solution)/shard_map/lpk,lkc->lpc/dot_general | solution.py:28
  52.1 2.3 %fusion.5 = f32[512,256]{0,1:T(8,128)S(1)} fusion(f32[512,256]{0,1:T(8,128)S(1)} %fusion.4, f32[512,128]{0,1:T(8,128)S(1)} %bitcast.55, f32[512,128]{0,1:T(8,128)S(1)} %bitcast.52, f32[512]{0:T(512)S(1)} %get-tuple-element.19, f32[512]{0:T(512)S(1)} %get-tuple-element.18, f32[1,512,512]{2,1,0:T(8,128)} %all-gather.4.cloned.1.call-done), kind=kOutput, calls=%fused_computation.11 | convolution fusion | flops 805961728 | bytes 2625536 | tf_op jit(solution)/shard_map/lpk,lkc->lpc/dot_general | solution.py:28
  54.4 3.1 %collective-permute-start = (f32[512,256]{0,1:T(8,128)S(1)}, f32[512,256]{0,1:T(8,128)S(1)}, u32[]{:S(2)}, u32[]{:S(2)}) collective-permute-start(f32[512,256]{0,1:T(8,128)S(1)} %fusion.5), channel_id=1, source_target_pairs={{0,4},{4,8},{8,12},{12,16},{16,20},{20,24},{24,28},{28,32},{32,36}... | collective-permute-start | bytes 1572872 | tf_op jit(solution)/shard_map/ppermute | solution.py:12
  57.5 0.9 constant_dynamic-slice_fusion
  58.4 4.7 %copy.23 = f32[2,128,128]{0,2,1:T(8,128)} copy(f32[2,128,128]{2,1,0:T(8,128)S(1)} %constant_dynamic-slice_fusion) | data formatting | bytes 262144
  63.1 1.8 gather_fusion.1
  64.9 0.6 negate_reduce_fusion
  65.5 113.5 %pmax.7 = f32[]{:T(128)} all-reduce(f32[]{:T(128)} %negate_reduce_fusion), channel_id=1, replica_groups=mesh['lvl'=128,'col'=4] {'lvl','col'}, use_global_device_ids=true, to_apply=%region_1.2 | all-reduce | flops 1 | bytes 8 | tf_op jit(solution)/shard_map/pmax | solution.py:55
  179.0 0.1 copy.20
  179.1 0.0 all-gather.6.cloned.1.call-done
  179.1 2.3 %convolution_bitcast_fusion.1 = f32[1,512,256]{1,2,0:T(8,128)S(1)} fusion(f32[512,256]{0,1:T(8,128)S(1)} %fusion.5, f32[1,512,512]{2,1,0:T(8,128)} %all-gather.6.cloned.1.call-done), kind=kOutput, calls=%fused_computation.3 | convolution fusion | flops 805306368 | bytes 2097152 | tf_op jit(solution)/shard_map/lpk,lkc->lpc/dot_general | solution.py:38
  181.4 0.0 all-gather.8.cloned.1.call-done
  181.5 0.0 collective-permute-done
  181.5 2.3 %convolution_bitcast_fusion = f32[1,512,256]{1,2,0:T(8,128)S(1)} fusion(f32[512,256]{0,1:T(8,128)S(1)} %collective-permute-done, f32[1,512,512]{2,1,0:T(8,128)} %all-gather.8.cloned.1.call-done), kind=kOutput, calls=%fused_computation.2 | convolution fusion | flops 805306368 | bytes 2097152 | tf_op jit(solution)/shard_map/lpk,lkc->lpc/dot_general | solution.py:45
  183.8 0.8 slice_divide_fusion
  184.5 0.8 copy.17
  185.4 0.8 copy.18
  186.2 0.8 copy.19
  (3 shorter events, 0.0 us)
Async XLA Ops:
  7.2 34.0 %all-gather.4.cloned.1.call-start = ((), (), s32[]{:S(2)}) async-start(), calls=%async_computation | async-start | bytes 1310720 | tf_op jit(solution)/shard_map/all_gather | solution.py:20
  9.0 170.1 %all-gather.6.cloned.1.call-start = ((), (), s32[]{:S(2)}) async-start(), calls=%async_computation.1 | async-start | bytes 1310720 | tf_op jit(solution)/shard_map/all_gather | solution.py:21
  10.8 170.6 %all-gather.8.cloned.1.call-start = ((), (), s32[]{:S(2)}) async-start(), calls=%async_computation.2 | async-start | bytes 1310720 | tf_op jit(solution)/shard_map/all_gather | solution.py:22
  54.4 127.1 %collective-permute-start = (f32[512,256]{0,1:T(8,128)S(1)}, f32[512,256]{0,1:T(8,128)S(1)}, u32[]{:S(2)}, u32[]{:S(2)}) collective-permute-start(f32[512,256]{0,1:T(8,128)S(1)} %fusion.5), channel_id=1, source_target_pairs={{0,4},{4,8},{8,12},{12,16},{16,20},{20,24},{24,28},{28,32},{32,36}... | collective-permute-start | bytes 1572872 | tf_op jit(solution)/shard_map/ppermute | solution.py:12
Sparse Core Ops, SparseCore 0:
  10.6 30.5 all-gather.3
  43.8 27.4 all-gather.5
  74.0 46.0 all-gather.7
where the time goes:
time: 197 us; the launch traced here: 194 us
  blocking collectives  114 us (58%)
  waiting for transfers between devices  28.3 us (14%)
  local copies, waits for them, and re-layouts  24.1 us (12%)
  between operations  13.9 us (7%)
  matrix products  9.16 us (5%)
  starting transfers between devices  3.22 us (2%)
    pmax x1, blocking collectives, per_device(): top_rate = lax.pmax(local_peak, ('lvl', 'col'))  114 us
    all_gather x1, waiting for transfers between devices, per_device(): lax.all_gather(odd_level, 'col', axis=2, tiled=True)  28.2 us
    gather x1, local copies, waits for them, and re-layouts, per_device(): out_rates = -jnp.diagonal(full_level, axis1=1, axis2=2)  8.54 us
    unnamed x7, local copies, waits for them, and re-layouts  7.57 us
    dot_general x2, matrix products, per_device(): jnp.einsum('lpk,lkc->lpc', full_level, solution, precision=lax.Precision....  4.6 us
  transfers between devices with their start and end apart: 4, of which 1 were waited for; matrix products, arithmetic and copies ran while one was open for 14% of the time, Pallas kernels for 0%

commit v1 on v0

v1 whole, which is shorter than its diff:
```python
import functools

import jax
import jax.numpy as jnp
from jax import lax
from jax.experimental import pallas as pl
from jax.experimental.pallas import tpu as pltpu
from jax.sharding import PartitionSpec as P

SWEEPS = 2
MESH = pl.DeviceIdType.MESH
F32 = jnp.float32
BF16 = jnp.bfloat16
CHUNKS = 4


def split(x):
    high = x.astype(BF16)
    low = (x - high.astype(F32)).astype(BF16)
    return high, low


def dot(a, b):
    return jnp.dot(a, b, preferred_element_type=F32)


def product(a_high, a_low, x):
    x_high, x_low = split(x)
    return dot(a_high, x_high) + (dot(a_high, x_low) + dot(a_low, x_high))


def kernel(
    sides,
    up,
    level,
    down,
    out_level,
    out_up,
    out_down,
    full,
    high,
    low,
    right,
    mine_even,
    squares,
    solved,
    below,
    upper,
    peaks,
    y_peaks,
    x_peaks,
    z_peaks,
    col_peaks,
    local_sem,
    link_send,
    link_recv,
    relay_send,
    relay_recv,
    own_send,
    own_recv,
    shift_send,
    shift_recv,
    y_send,
    y_recv,
    x_send,
    x_recv,
    z_send,
    z_recv,
    col_send,
    col_recv,
):
    ny, nz, nx = sides
    levels = ny * nz * nx
    lvl = lax.axis_index("lvl")
    col = lax.axis_index("col")
    rows, share = up.shape[1], up.shape[2]
    x = lax.rem(lvl, nx)
    z = lax.rem(lvl // nx, nz)
    y = lvl // (nx * nz)
    partner = col + 1 - 2 * lax.rem(col, 2)
    across = lax.rem(col + 2, 4)

    def at(yy, zz, xx):
        return (yy * nz + zz) * nx + xx

    y_group = [(at(lax.rem(y + j, ny), z, x), col) for j in range(1, ny)]
    x_group = [(at(y, z, lax.rem(x + j, nx)), col) for j in range(1, nx)]
    z_group = [(at(y, lax.rem(z + j, nz), x), col) for j in range(1, nz)]
    col_group = [(lvl, lax.rem(col + j, 4)) for j in range(1, 4)]
    above = lax.rem(lvl + 1, levels)
    beneath = lax.rem(lvl + levels - 1, levels)

    def columns(c):
        return pl.ds(pl.multiple_of(c * share, share), share)

    mine = columns(col)
    theirs = columns(across)
    blocks = (level.at[1], up.at[0], down.at[0])

    local = [
        pltpu.make_async_copy(level.at[0, mine, :], squares.at[0], local_sem.at[0]),
        pltpu.make_async_copy(level.at[1, mine, :], squares.at[1], local_sem.at[1]),
        pltpu.make_async_copy(up.at[1], right.at[:, 0:share], local_sem.at[2]),
        pltpu.make_async_copy(down.at[1], right.at[:, share : 2 * share], local_sem.at[3]),
        pltpu.make_async_copy(level.at[0], mine_even, local_sem.at[4]),
    ] + [
        pltpu.make_async_copy(blocks[m], full.at[m, :, mine], local_sem.at[5 + m]) for m in range(3)
    ]
    for copy in local:
        copy.start()

    barrier = pltpu.get_barrier_semaphore()
    greeted = y_group + x_group + z_group + col_group + [(above, col), (beneath, col)]
    for device in greeted:
        pl.semaphore_signal(barrier, inc=1, device_id=device, device_id_type=MESH)

    local[0].wait()
    local[1].wait()
    row = lax.broadcasted_iota(jnp.int32, (share, share), 0)
    column = lax.broadcasted_iota(jnp.int32, (share, share), 1)
    diagonal = row == column
    rates = jnp.where(diagonal, jnp.maximum(-squares[0], -squares[1]), -jnp.inf)
    peaks[0] = jnp.max(rates.reshape(share // 8, 8, share), axis=0)

    pl.semaphore_wait(barrier, len(greeted))

    def send_peaks(stage, group, slots, send, recv):
        copies = []
        for j, device in enumerate(group):
            copies.append(
                pltpu.make_async_remote_copy(
                    src_ref=peaks.at[stage],
                    dst_ref=slots.at[j],
                    send_sem=send.at[j],
                    recv_sem=recv.at[j],
                    device_id=device,
                    device_id_type=MESH,
                )
            )
            copies[-1].start()
        return copies

    def take_peaks(stage, copies, slots):
        best = peaks[stage]
        for j, copy in enumerate(copies):
            copy.wait_recv()
            best = jnp.maximum(best, slots[j])
        peaks[stage + 1] = best

    step = rows // CHUNKS

    def link(m, i):
        part = pl.ds(i * step, step)
        return pltpu.make_async_remote_copy(
            src_ref=blocks[m].at[part, :],
            dst_ref=full.at[m, part, mine],
            send_sem=link_send.at[m, i],
            recv_sem=link_recv.at[m, i],
            device_id=(lvl, across),
            device_id_type=MESH,
        )

    def relay(m, i):
        part = pl.ds(i * step, step)
        return pltpu.make_async_remote_copy(
            src_ref=full.at[m, part, theirs],
            dst_ref=full.at[m, part, theirs],
            send_sem=relay_send.at[m, i],
            recv_sem=relay_recv.at[m, i],
            device_id=(lvl, partner),
            device_id_type=MESH,
        )

    def own(m):
        return pltpu.make_async_remote_copy(
            src_ref=blocks[m],
            dst_ref=full.at[m, :, mine],
            send_sem=own_send.at[m],
            recv_sem=own_recv.at[m],
            device_id=(lvl, partner),
            device_id_type=MESH,
        )

    col_copies = send_peaks(0, col_group, col_peaks, col_send, col_recv)
    links = [[link(m, i) for i in range(CHUNKS)] for m in range(3)]
    relays = [[relay(m, i) for i in range(CHUNKS)] for m in range(3)]
    owns = [own(m) for m in range(3)]
    for i in range(CHUNKS):
        links[0][i].start()
    owns[0].start()
    for i in range(CHUNKS):
        links[1][i].start()
    owns[1].start()
    take_peaks(0, col_copies, col_peaks)
    y_copies = send_peaks(1, y_group, y_peaks, y_send, y_recv)

    def hand_on(m, i):
        links[m][i].wait_recv()
        relays[m][i].start()

    def gathered(m):
        local[5 + m].wait()
        owns[m].wait_recv()
        for i in range(CHUNKS):
            relays[m][i].wait_recv()

    for i in range(CHUNKS):
        hand_on(0, i)
    take_peaks(1, y_copies, y_peaks)
    x_copies = send_peaks(2, x_group, x_peaks, x_send, x_recv)
    gathered(0)
    local[2].wait()
    local[3].wait()

    inverse = []
    for s in range(rows // share):
        part = slice(s * share, (s + 1) * share)
        square = full[0, part, part]
        inverse.append(1.0 / jnp.sum(jnp.where(diagonal, -square, 0.0), axis=1, keepdims=True))
        high[0, part, :], low[0, part, :] = split(full[0, part, :])
        high[0, part, part], low[0, part, part] = split(jnp.where(diagonal, 0.0, square))
    inverse = jnp.concatenate(inverse, axis=0)
    side = right[...]
    guess = side * inverse
    for _ in range(SWEEPS - 1):
        guess = (side + product(high[0], low[0], guess)) * inverse
    solved[...] = (side + product(high[0], low[0], guess)) * inverse

    shift = pltpu.make_async_remote_copy(
        src_ref=solved,
        dst_ref=below,
        send_sem=shift_send.at[0],
        recv_sem=shift_recv.at[0],
        device_id=(above, col),
        device_id_type=MESH,
    )

    @pl.when(lvl < levels - 1)
    def _():
        shift.start()

    take_peaks(2, x_copies, x_peaks)
    z_copies = send_peaks(3, z_group, z_peaks, z_send, z_recv)
    for i in range(CHUNKS):
        links[2][i].start()
    owns[2].start()
    for i in range(CHUNKS):
        hand_on(1, i)
    gathered(1)
    u_high, u_low = split(full[1])
    upper[...] = product(u_high, u_low, solved[...])

    for i in range(CHUNKS):
        hand_on(2, i)
    gathered(2)
    w_high, w_low = split(full[2])
    high[1] = w_high
    low[1] = w_low
    take_peaks(3, z_copies, z_peaks)
    scale = 1.0 / jnp.max(peaks[4], keepdims=True)[0:1, 0:1]
    local[4].wait()

    @pl.when(lvl > 0)
    def _():
        shift.wait_recv()

    @pl.when(lvl == 0)
    def _():
        below[...] = jnp.zeros_like(below)

    lower = product(high[1], low[1], below[...])
    out_level[0] = (mine_even[...] + upper[:, share:] + lower[:, :share]) * scale
    out_up[0] = upper[:, :share] * scale
    out_down[0] = lower[:, share:] * scale

    for copy in col_copies + y_copies + x_copies + z_copies + owns:
        copy.wait_send()
    for m in range(3):
        for i in range(CHUNKS):
            links[m][i].wait_send()
            relays[m][i].wait_send()

    @pl.when(lvl < levels - 1)
    def _():
        shift.wait_send()


def per_device(sides, up, level, down):
    rows, share = up.shape[1], up.shape[2]
    ny, nz, nx = sides
    block = jax.ShapeDtypeStruct((1, rows, share), F32)
    dma = pltpu.SemaphoreType.DMA
    tile = (8, share)
    return pl.pallas_call(
        functools.partial(kernel, sides),
        out_shape=(block, block, block),
        in_specs=[pl.BlockSpec(memory_space=pl.ANY)] * 3,
        out_specs=(pl.BlockSpec(memory_space=pltpu.VMEM),) * 3,
        scratch_shapes=[
            pltpu.VMEM((3, rows, rows), F32),
            pltpu.VMEM((2, rows, rows), BF16),
            pltpu.VMEM((2, rows, rows), BF16),
            pltpu.VMEM((rows, 2 * share), F32),
            pltpu.VMEM((rows, share), F32),
            pltpu.VMEM((2, share, share), F32),
            pltpu.VMEM((rows, 2 * share), F32),
            pltpu.VMEM((rows, 2 * share), F32),
            pltpu.VMEM((rows, 2 * share), F32),
            pltpu.VMEM((5,) + tile, F32),
            pltpu.VMEM((ny - 1,) + tile, F32),
            pltpu.VMEM((nx - 1,) + tile, F32),
            pltpu.VMEM((nz - 1,) + tile, F32),
            pltpu.VMEM((3,) + tile, F32),
            dma((8,)),
            dma((3, CHUNKS)),
            dma((3, CHUNKS)),
            dma((3, CHUNKS)),
            dma((3, CHUNKS)),
            dma((3,)),
            dma((3,)),
            dma((1,)),
            dma((1,)),
            dma((ny - 1,)),
            dma((ny - 1,)),
            dma((nx - 1,)),
            dma((nx - 1,)),
            dma((nz - 1,)),
            dma((nz - 1,)),
            dma((3,)),
            dma((3,)),
        ],
        compiler_params=pltpu.CompilerParams(
            collective_id=0, has_side_effects=True, vmem_limit_bytes=40 * 1024 * 1024
        ),
    )(up, level, down)


def solution(mesh, sides=(8, 4, 4)):
    placed = P("lvl", None, "col")
    return jax.shard_map(
        functools.partial(per_device, sides),
        mesh=mesh,
        in_specs=(placed, placed, placed),
        out_specs=(placed, placed, placed),
        check_vma=False,
    )
```

time: 197 us -> 61 us (0.31)
  the two profiles are of different devices: /device:TPU:57 before, /device:TPU:79 now
where the time goes in v1:
time: 61 us; the launch traced here: 60.7 us
  Pallas kernels  54.8 us (90%)
  local copies, waits for them, and re-layouts  5.23 us (9%)
  between operations  0.65 us (1%)
    pallas_call x1, Pallas kernels, per_device(): pl.pallas_call(functools.partial(kernel, sides), out_shape=(block, block,...  54.8 us
    unnamed x9, local copies, waits for them, and re-layouts  5.23 us

profile of v1, /device:TPU:79, one launch (start us, length us, event | category | flops | bytes accessed | tf_op | source)
XLA Modules:
  0.0 60.7 jit_solution(10409286818994543443)
XLA Ops:
  0.6 0.0 copy-start
  0.6 1.0 %copy-done = f32[2,512,128]{2,1,0:T(8,128)S(1)} copy-done((f32[2,512,128]{2,1,0:T(8,128)S(1)}, f32[2,512,128]{2,1,0:T(8,128)}, u32[]{:S(2)}) %copy-start) | copy-done | bytes 524312
  1.7 0.0 copy-start.1
  1.7 1.0 %copy-done.1 = f32[2,512,128]{2,1,0:T(8,128)S(1)} copy-done((f32[2,512,128]{2,1,0:T(8,128)S(1)}, f32[2,512,128]{2,1,0:T(8,128)}, u32[]{:S(2)}) %copy-start.1) | copy-done | bytes 524312
  2.7 0.0 copy-start.2
  2.7 1.0 %copy-done.2 = f32[2,512,128]{2,1,0:T(8,128)S(1)} copy-done((f32[2,512,128]{2,1,0:T(8,128)S(1)}, f32[2,512,128]{2,1,0:T(8,128)}, u32[]{:S(2)}) %copy-start.2) | copy-done | bytes 524312
  3.8 54.8 %shard_map.58 = (f32[1,512,128]{2,1,0:T(8,128)S(1)}, f32[1,512,128]{2,1,0:T(8,128)S(1)}, f32[1,512,128]{2,1,0:T(8,128)S(1)}) custom-call(f32[2,512,128]{2,1,0:T(8,128)S(1)} %copy-done, f32[2,512,128]{2,1,0:T(8,128)S(1)} %copy-done.1, f32[2,512,128]{2,1,0:T(8,128)S(1)} %copy-done.2), custom_call_target="tpu_custom_call" | custom-call | tf_op jit(solution)/shard_map/pallas_call | solution.py:294
  58.6 0.7 %copy.9 = f32[1,512,128]{2,1,0:T(8,128)} copy(f32[1,512,128]{2,1,0:T(8,128)S(1)} %get-tuple-element.6) | data formatting | bytes 524288
  59.3 0.7 %copy.10 = f32[1,512,128]{2,1,0:T(8,128)} copy(f32[1,512,128]{2,1,0:T(8,128)S(1)} %get-tuple-element.7) | data formatting | bytes 524288
  60.0 0.7 %copy.11 = f32[1,512,128]{2,1,0:T(8,128)} copy(f32[1,512,128]{2,1,0:T(8,128)S(1)} %get-tuple-element.8) | data formatting | bytes 524288
Async XLA Ops:
  0.6 1.0 %copy-start = (f32[2,512,128]{2,1,0:T(8,128)S(1)}, f32[2,512,128]{2,1,0:T(8,128)}, u32[]{:S(2)}) copy-start(f32[2,512,128]{2,1,0:T(8,128)} %up.1) | copy-start | bytes 1572868
  1.7 1.0 %copy-start.1 = (f32[2,512,128]{2,1,0:T(8,128)S(1)}, f32[2,512,128]{2,1,0:T(8,128)}, u32[]{:S(2)}) copy-start(f32[2,512,128]{2,1,0:T(8,128)} %level.1) | copy-start | bytes 1572868
  2.7 1.0 %copy-start.2 = (f32[2,512,128]{2,1,0:T(8,128)S(1)}, f32[2,512,128]{2,1,0:T(8,128)}, u32[]{:S(2)}) copy-start(f32[2,512,128]{2,1,0:T(8,128)} %down.1) | copy-start | bytes 1572868

commit v2 on v1

--- a/solution.py
+++ b/solution.py
@@ -27,6 +27,10 @@
 def product(a_high, a_low, x):
     x_high, x_low = split(x)
     return dot(a_high, x_high) + (dot(a_high, x_low) + dot(a_low, x_high))
+
+
+def start_rank(y, ny):
+    return jnp.where(y == 0, 0, jnp.where(2 * y <= ny, 2 * y - 1, 2 * (ny - y)))
 
 
 def kernel(
@@ -45,12 +49,13 @@
     squares,
     solved,
     below,
+    hop,
     upper,
     peaks,
+    col_peaks,
+    x_peaks,
     y_peaks,
-    x_peaks,
     z_peaks,
-    col_peaks,
     local_sem,
     link_send,
     link_recv,
@@ -60,35 +65,52 @@
     own_recv,
     shift_send,
     shift_recv,
+    hop_send,
+    hop_recv,
+    forward_send,
+    col_send,
+    col_recv,
+    x_send,
+    x_recv,
     y_send,
     y_recv,
-    x_send,
-    x_recv,
     z_send,
     z_recv,
-    col_send,
-    col_recv,
+    x_ack,
+    y_ack,
+    z_ack,
+    next_ack,
 ):
     ny, nz, nx = sides
-    levels = ny * nz * nx
     lvl = lax.axis_index("lvl")
     col = lax.axis_index("col")
     rows, share = up.shape[1], up.shape[2]
     x = lax.rem(lvl, nx)
-    z = lax.rem(lvl // nx, nz)
-    y = lvl // (nx * nz)
-    partner = col + 1 - 2 * lax.rem(col, 2)
+    run = lvl // nx
+    runs = ny * nz
+    z = lax.rem(run, nz)
+    y = run // nz
+    core = lax.rem(col, 2)
+    side = col // 2
+    partner = col + 1 - 2 * core
     across = lax.rem(col + 2, 4)
 
     def at(yy, zz, xx):
         return (yy * nz + zz) * nx + xx
 
-    y_group = [(at(lax.rem(y + j, ny), z, x), col) for j in range(1, ny)]
-    x_group = [(at(y, z, lax.rem(x + j, nx)), col) for j in range(1, nx)]
-    z_group = [(at(y, lax.rem(z + j, nz), x), col) for j in range(1, nz)]
+    def signal(semaphore, device):
+        pl.semaphore_signal(semaphore, inc=1, device_id=device, device_id_type=MESH)
+
+    rank = start_rank(y, ny)
+    x_group = [lax.rem(x + j, nx) for j in range(1, nx)]
+    y_group = [lax.rem(y + j, ny) for j in range(1, ny)]
+    z_group = [lax.rem(z + j, nz) for j in range(1, nz)]
+    x_devices = [(at(y, z, xx), col) for xx in x_group]
+    y_devices = [(at(yy, z, x), col) for yy in y_group]
     col_group = [(lvl, lax.rem(col + j, 4)) for j in range(1, 4)]
-    above = lax.rem(lvl + 1, levels)
-    beneath = lax.rem(lvl + levels - 1, levels)
+    head = (run + 1) * nx
+    turns = run < runs - 1
+    last = x == nx - 1
 
     def columns(c):
         return pl.ds(pl.multiple_of(c * share, share), share)
@@ -106,13 +128,39 @@
     ] + [
         pltpu.make_async_copy(blocks[m], full.at[m, :, mine], local_sem.at[5 + m]) for m in range(3)
     ]
+
+    barrier = pltpu.get_barrier_semaphore()
+    for device in col_group:
+        signal(barrier, device)
     for copy in local:
         copy.start()
-
-    barrier = pltpu.get_barrier_semaphore()
-    greeted = y_group + x_group + z_group + col_group + [(above, col), (beneath, col)]
-    for device in greeted:
-        pl.semaphore_signal(barrier, inc=1, device_id=device, device_id_type=MESH)
+    for xx, device in zip(x_group, x_devices):
+
+        @pl.when(xx > x)
+        def _():
+            signal(barrier, device)
+
+    for yy, device in zip(y_group, y_devices):
+
+        @pl.when(start_rank(yy, ny) > rank)
+        def _():
+            signal(barrier, device)
+
+    for zz in z_group:
+
+        @pl.when(zz > z)
+        def _():
+            for half in range(2):
+                signal(barrier, (at(y, zz, x), half * 2 + core))
+
+    @pl.when(turns & (z < nz - 1))
+    def _():
+        signal(barrier, (head, col))
+
+    @pl.when((x == 0) & (z == 0) & (run > 0))
+    def _():
+        for xx in range(nx):
+            signal(barrier, (lvl - nx + xx, col))
 
     local[0].wait()
     local[1].wait()
@@ -122,7 +170,10 @@
     rates = jnp.where(diagonal, jnp.maximum(-squares[0], -squares[1]), -jnp.inf)
     peaks[0] = jnp.max(rates.reshape(share // 8, 8, share), axis=0)
 
-    pl.semaphore_wait(barrier, len(greeted))
+    expected = 3 + x + rank + 2 * z
+    expected = expected + jnp.where((x == 0) & (z > 0), nx, 0)
+    expected = expected + jnp.where(turns & (z == nz - 1), 1, 0)
+    pl.semaphore_wait(barrier, expected)
 
     def send_peaks(stage, group, slots, send, recv):
         copies = []
@@ -181,18 +232,39 @@
             device_id_type=MESH,
         )
 
-    col_copies = send_peaks(0, col_group, col_peaks, col_send, col_recv)
     links = [[link(m, i) for i in range(CHUNKS)] for m in range(3)]
     relays = [[relay(m, i) for i in range(CHUNKS)] for m in range(3)]
     owns = [own(m) for m in range(3)]
-    for i in range(CHUNKS):
-        links[0][i].start()
-    owns[0].start()
-    for i in range(CHUNKS):
-        links[1][i].start()
-    owns[1].start()
-    take_peaks(0, col_copies, col_peaks)
-    y_copies = send_peaks(1, y_group, y_peaks, y_send, y_recv)
+
+    col_copies = send_peaks(0, col_group, col_peaks, col_send, col_recv)
+    for m in range(3):
+        for i in range(CHUNKS):
+            links[m][i].start()
+        owns[m].start()
+
+    for xx, device in zip(x_group, x_devices):
+
+        @pl.when(xx < x)
+        def _():
+            signal(x_ack, device)
+
+    for yy, device in zip(y_group, y_devices):
+
+        @pl.when(start_rank(yy, ny) < rank)
+        def _():
+            signal(y_ack, device)
+
+    for zz in z_group:
+
+        @pl.when(zz < z)
+        def _():
+            for half in range(2):
+                signal(z_ack, (at(y, zz, x), half * 2 + core))
+
+    @pl.when((x == 0) & (z > 0))
+    def _():
+        for xx in range(nx):
+            signal(next_ack, (lvl - nx + xx, col))
 
     def hand_on(m, i):
         links[m][i].wait_recv()
@@ -204,10 +276,22 @@
         for i in range(CHUNKS):
             relays[m][i].wait_recv()
 
+    take_peaks(0, col_copies, col_peaks)
+
+    @pl.when(x < nx - 1)
+    def _():
+        pl.semaphore_wait(x_ack, nx - 1 - x)
+
+    x_copies = send_peaks(1, x_devices, x_peaks, x_send, x_recv)
     for i in range(CHUNKS):
         hand_on(0, i)
-    take_peaks(1, y_copies, y_peaks)
-    x_copies = send_peaks(2, x_group, x_peaks, x_send, x_recv)
+    take_peaks(1, x_copies, x_peaks)
+
+    @pl.when(rank < ny - 1)
+    def _():
+        pl.semaphore_wait(y_ack, ny - 1 - rank)
+
+    y_copies = send_peaks(2, y_devices, y_peaks, y_send, y_recv)
     gathered(0)
     local[2].wait()
     local[3].wait()
@@ -219,31 +303,110 @@
         inverse.append(1.0 / jnp.sum(jnp.where(diagonal, -square, 0.0), axis=1, keepdims=True))
         high[0, part, :], low[0, part, :] = split(full[0, part, :])
         high[0, part, part], low[0, part, part] = split(jnp.where(diagonal, 0.0, square))
-    inverse = jnp.concatenate(inverse, axis=0)
-    side = right[...]
-    guess = side * inverse
+    every = jnp.concatenate(inverse, axis=0)
+    sides_of = right[...]
+    guess = sides_of * every
     for _ in range(SWEEPS - 1):
-        guess = (side + product(high[0], low[0], guess)) * inverse
-    solved[...] = (side + product(high[0], low[0], guess)) * inverse
-
-    shift = pltpu.make_async_remote_copy(
-        src_ref=solved,
-        dst_ref=below,
-        send_sem=shift_send.at[0],
-        recv_sem=shift_recv.at[0],
-        device_id=(above, col),
-        device_id_type=MESH,
-    )
-
-    @pl.when(lvl < levels - 1)
-    def _():
-        shift.start()
-
-    take_peaks(2, x_copies, x_peaks)
-    z_copies = send_peaks(3, z_group, z_peaks, z_send, z_recv)
-    for i in range(CHUNKS):
-        links[2][i].start()
-    owns[2].start()
+        guess = (sides_of + product(high[0], low[0], guess)) * every
+    guess_high, guess_low = split(guess)
+
+    def piece(q):
+        return pl.ds(pl.multiple_of(q * share, share), share)
+
+    def shift(source, q, device):
+        return pltpu.make_async_remote_copy(
+            src_ref=source,
+            dst_ref=below.at[piece(q), :],
+            send_sem=shift_send.at[q],
+            recv_sem=shift_recv.at[q],
+            device_id=(device, col),
+            device_id_type=MESH,
+        )
+
+    def forward():
+        return pltpu.make_async_remote_copy(
+            src_ref=hop,
+            dst_ref=below.at[piece(x + 1), :],
+            send_sem=forward_send.at[0],
+            recv_sem=shift_recv.at[x + 1],
+            device_id=(head, col),
+            device_id_type=MESH,
+        )
+
+    def detour(q):
+        return pltpu.make_async_remote_copy(
+            src_ref=solved.at[piece(q), :],
+            dst_ref=hop,
+            send_sem=hop_send.at[q - 1],
+            recv_sem=hop_recv.at[0],
+            device_id=(at(y, z, q - 1), col),
+            device_id_type=MESH,
+        )
+
+    @pl.when(turns & (z < nz - 1))
+    def _():
+        pl.semaphore_wait(next_ack, 1)
+
+    pieces = rows // share
+    for q in range(pieces):
+        part = slice(q * share, (q + 1) * share)
+        term = dot(high[0, part, :], guess_high) + (
+            dot(high[0, part, :], guess_low) + dot(low[0, part, :], guess_high)
+        )
+        solved[part, :] = (right[part, :] + term) * inverse[q]
+
+        if q == 0:
+
+            @pl.when(jnp.logical_not(last) | turns)
+            def _():
+                shift(solved.at[piece(0), :], 0, lvl + 1).start()
+        else:
+
+            @pl.when(jnp.logical_not(last))
+            def _():
+                shift(solved.at[piece(q), :], q, lvl + 1).start()
+
+            @pl.when(last & turns)
+            def _():
+                detour(q).start()
+
+    take_peaks(2, y_copies, y_peaks)
+
+    @pl.when(z < nz - 1)
+    def _():
+        pl.semaphore_wait(z_ack, 2 * (nz - 1 - z))
+
+
+    def z_copy(slot, zz, half, sender):
+        return pltpu.make_async_remote_copy(
+            src_ref=peaks.at[3],
+            dst_ref=z_peaks.at[slot],
+            send_sem=z_send.at[sender],
+            recv_sem=z_recv.at[slot],
+            device_id=(at(y, lax.rem(zz + nz, nz), x), half * 2 + core),
+            device_id_type=MESH,
+        )
+
+    ahead = [z_copy(slot, z + slot + 1, half, 2 * slot + half) for slot in range(2) for half in range(2)]
+    behind = [z_copy(2, z - 1, half, half) for half in range(2)]
+
+    @pl.when(side == 1)
+    def _():
+        for copy in ahead:
+            copy.start()
+
+    @pl.when(side == 0)
+    def _():
+        for copy in behind:
+            copy.start()
+
+    hands_over = jnp.logical_not(last) & turns
+
+    @pl.when(hands_over)
+    def _():
+        detour(1).wait_recv()
+        forward().start()
+
     for i in range(CHUNKS):
         hand_on(1, i)
     gathered(1)
@@ -256,41 +419,74 @@
     w_high, w_low = split(full[2])
     high[1] = w_high
     low[1] = w_low
-    take_peaks(3, z_copies, z_peaks)
-    scale = 1.0 / jnp.max(peaks[4], keepdims=True)[0:1, 0:1]
     local[4].wait()
 
-    @pl.when(lvl > 0)
-    def _():
-        shift.wait_recv()
-
     @pl.when(lvl == 0)
     def _():
         below[...] = jnp.zeros_like(below)
 
-    lower = product(high[1], low[1], below[...])
-    out_level[0] = (mine_even[...] + upper[:, share:] + lower[:, :share]) * scale
-    out_up[0] = upper[:, :share] * scale
-    out_down[0] = lower[:, share:] * scale
-
-    for copy in col_copies + y_copies + x_copies + z_copies + owns:
+    lower = 0.0
+    for half in range(2):
+        part = slice(half * rows // 2, (half + 1) * rows // 2)
+
+        @pl.when(lvl > 0)
+        def _():
+            for q in range(half * pieces // 2, (half + 1) * pieces // 2):
+                shift(solved.at[piece(q), :], q, lvl).wait_recv()
+
+        lower = lower + product(high[1, :, part], low[1, :, part], below[part, :])
+    best = peaks[3]
+    for slot in range(3):
+        z_copy(slot, z, side, 0).wait_recv()
+        best = jnp.maximum(best, z_peaks[slot])
+    factor = 1.0 / jnp.max(best, keepdims=True)
+    out_level[0] = (mine_even[...] + upper[:, share:] + lower[:, :share]) * factor
+    out_up[0] = upper[:, :share] * factor
+    out_down[0] = lower[:, share:] * factor
+
+    for copy in col_copies + x_copies + y_copies + owns:
         copy.wait_send()
     for m in range(3):
         for i in range(CHUNKS):
             links[m][i].wait_send()
             relays[m][i].wait_send()
 
-    @pl.when(lvl < levels - 1)
-    def _():
-        shift.wait_send()
+    @pl.when(side == 1)
+    def _():
+        for copy in ahead:
+            copy.wait_send()
+
+    @pl.when(side == 0)
+    def _():
+        for copy in behind:
+            copy.wait_send()
+
+    @pl.when(jnp.logical_not(last) | turns)
+    def _():
+        shift(solved.at[piece(0), :], 0, lvl).wait_send()
+
+    @pl.when(jnp.logical_not(last))
+    def _():
+        for q in range(1, pieces):
+            shift(solved.at[piece(q), :], q, lvl).wait_send()
+
+    @pl.when(last & turns)
+    def _():
+        for q in range(1, pieces):
+            detour(q).wait_send()
+
+    @pl.when(hands_over)
+    def _():
+        forward().wait_send()
 
 
 def per_device(sides, up, level, down):
     rows, share = up.shape[1], up.shape[2]
     ny, nz, nx = sides
+    dma = pltpu.SemaphoreType.DMA
+    regular = pltpu.SemaphoreType.REGULAR
+    tile = (8, share)
     block = jax.ShapeDtypeStruct((1, rows, share), F32)
-    dma = pltpu.SemaphoreType.DMA
-    tile = (8, share)
     return pl.pallas_call(
         functools.partial(kernel, sides),
         out_shape=(block, block, block),
@@ -305,11 +501,12 @@
             pltpu.VMEM((2, share, share), F32),
             pltpu.VMEM((rows, 2 * share), F32),
             pltpu.VMEM((rows, 2 * share), F32),
+            pltpu.VMEM((share, 2 * share), F32),
             pltpu.VMEM((rows, 2 * share), F32),
-            pltpu.VMEM((5,) + tile, F32),
+            pltpu.VMEM((4,) + tile, F32),
+            pltpu.VMEM((3,) + tile, F32),
+            pltpu.VMEM((nx - 1,) + tile, F32),
             pltpu.VMEM((ny - 1,) + tile, F32),
-            pltpu.VMEM((nx - 1,) + tile, F32),
-            pltpu.VMEM((nz - 1,) + tile, F32),
             pltpu.VMEM((3,) + tile, F32),
             dma((8,)),
             dma((3, CHUNKS)),
@@ -318,19 +515,26 @@
             dma((3, CHUNKS)),
             dma((3,)),
             dma((3,)),
+            dma((rows // share,)),
+            dma((rows // share,)),
+            dma((nx - 1,)),
             dma((1,)),
             dma((1,)),
+            dma((3,)),
+            dma((3,)),
+            dma((nx - 1,)),
+            dma((nx - 1,)),
             dma((ny - 1,)),
             dma((ny - 1,)),
-            dma((nx - 1,)),
-            dma((nx - 1,)),
-            dma((nz - 1,)),
-            dma((nz - 1,)),
+            dma((4,)),
             dma((3,)),
-            dma((3,)),
+            regular,
+            regular,
+            regular,
+            regular,
         ],
         compiler_params=pltpu.CompilerParams(
-            collective_id=0, has_side_effects=True, vmem_limit_bytes=40 * 1024 * 1024
+            collective_id=0, has_side_effects=True, vmem_limit_bytes=62 * 1024 * 1024
         ),
     )(up, level, down)
 

time: 61 us -> 47.5 us (0.78)
  the two profiles are of different devices: /device:TPU:79 before, /device:TPU:57 now
where the time goes in v2:
time: 47.5 us; the launch traced here: 46.9 us
  Pallas kernels  42.8 us (90%)
  local copies, waits for them, and re-layouts  3.46 us (7%)
  between operations  0.65 us (1%)
    pallas_call x1, Pallas kernels, per_device(): pl.pallas_call(functools.partial(kernel, sides), out_shape=(block, block,...  42.8 us
    unnamed x7, local copies, waits for them, and re-layouts  3.46 us

profile of v2, /device:TPU:57, one launch (start us, length us, event | category | flops | bytes accessed | tf_op | source)
XLA Modules:
  0.0 46.9 jit_solution(14454499246131529029)
XLA Ops:
  0.6 42.8 %shard_map.58 = (f32[1,512,128]{2,1,0:T(8,128)}, f32[1,512,128]{2,1,0:T(8,128)}, f32[1,512,128]{2,1,0:T(8,128)}) custom-call(f32[2,512,128]{2,1,0:T(8,128)} %up.1, f32[2,512,128]{2,1,0:T(8,128)} %level.1, f32[2,512,128]{2,1,0:T(8,128)} %down.1), custom_call_target="tpu_custom_call" | custom-call | tf_op jit(solution)/shard_map/pallas_call | solution.py:490
  43.4 0.0 copy-start.1
  43.4 1.7 %copy.9 = f32[1,512,128]{2,1,0:T(8,128)} copy(f32[1,512,128]{2,1,0:T(8,128)} %get-tuple-element.6) | data formatting | bytes 524288
  45.1 0.0 copy-done.1
  45.1 0.0 copy-start
  45.1 0.7 %copy.10 = f32[1,512,128]{2,1,0:T(8,128)} copy(f32[1,512,128]{2,1,0:T(8,128)S(1)} %copy-done.1) | data formatting | bytes 524288
  45.8 0.3 copy-done
  46.2 0.7 %copy.11 = f32[1,512,128]{2,1,0:T(8,128)} copy(f32[1,512,128]{2,1,0:T(8,128)S(1)} %copy-done) | data formatting | bytes 524288
Async XLA Ops:
  43.4 1.7 %copy-start.1 = (f32[1,512,128]{2,1,0:T(8,128)S(1)}, f32[1,512,128]{2,1,0:T(8,128)}, u32[]{:S(2)}) copy-start(f32[1,512,128]{2,1,0:T(8,128)} %get-tuple-element.7) | copy-start | bytes 786436
  45.1 1.0 %copy-start = (f32[1,512,128]{2,1,0:T(8,128)S(1)}, f32[1,512,128]{2,1,0:T(8,128)}, u32[]{:S(2)}) copy-start(f32[1,512,128]{2,1,0:T(8,128)} %get-tuple-element.8) | copy-start | bytes 786436

commit v3 on v2

--- a/solution.py
+++ b/solution.py
@@ -12,6 +12,14 @@
 F32 = jnp.float32
 BF16 = jnp.bfloat16
 CHUNKS = 4
+EARLY = 1
+UNIT = 64
+STRAIGHT = -1
+LATE_ROUTES = (-1, -1, -1, -1, 0, 0, 2, 2)
+
+
+def slot_of(u):
+    return sum(LATE_ROUTES[v] == LATE_ROUTES[u] for v in range(u))
 
 
 def split(x):
@@ -29,8 +37,13 @@
     return dot(a_high, x_high) + (dot(a_high, x_low) + dot(a_low, x_high))
 
 
-def start_rank(y, ny):
-    return jnp.where(y == 0, 0, jnp.where(2 * y <= ny, 2 * y - 1, 2 * (ny - y)))
+def start_rank(y, ny, first_last):
+    rank = jnp.where(y == 0, 0, jnp.where(2 * y <= ny, 2 * y - 1, 2 * (ny - y)))
+    return jnp.where(first_last, jnp.where(y == 0, ny - 1, rank - 1), rank)
+
+
+def x_rank(x, nx, first_last):
+    return jnp.where(first_last, jnp.where(x == 0, nx - 1, x - 1), x)
 
 
 def kernel(
@@ -65,7 +78,6 @@
     own_recv,
     shift_send,
     shift_recv,
-    hop_send,
     hop_recv,
     forward_send,
     col_send,
@@ -101,7 +113,10 @@
     def signal(semaphore, device):
         pl.semaphore_signal(semaphore, inc=1, device_id=device, device_id_type=MESH)
 
-    rank = start_rank(y, ny)
+    y_late = (x == 0) & (z == 0) & (col == 0)
+    x_late = (y == 0) & (z == 0) & (col == 0)
+    rank = start_rank(y, ny, y_late)
+    place = x_rank(x, nx, x_late)
     x_group = [lax.rem(x + j, nx) for j in range(1, nx)]
     y_group = [lax.rem(y + j, ny) for j in range(1, ny)]
     z_group = [lax.rem(z + j, nz) for j in range(1, nz)]
@@ -111,6 +126,7 @@
     head = (run + 1) * nx
     turns = run < runs - 1
     last = x == nx - 1
+    holds = (z == nz - 1) & turns & ((x != 1) | (1 in LATE_ROUTES))
 
     def columns(c):
         return pl.ds(pl.multiple_of(c * share, share), share)
@@ -136,13 +152,13 @@
         copy.start()
     for xx, device in zip(x_group, x_devices):
 
-        @pl.when(xx > x)
+        @pl.when(x_rank(xx, nx, x_late) > place)
         def _():
             signal(barrier, device)
 
     for yy, device in zip(y_group, y_devices):
 
-        @pl.when(start_rank(yy, ny) > rank)
+        @pl.when(start_rank(yy, ny, y_late) > rank)
         def _():
             signal(barrier, device)
 
@@ -170,7 +186,7 @@
     rates = jnp.where(diagonal, jnp.maximum(-squares[0], -squares[1]), -jnp.inf)
     peaks[0] = jnp.max(rates.reshape(share // 8, 8, share), axis=0)
 
-    expected = 3 + x + rank + 2 * z
+    expected = 3 + place + rank + 2 * z
     expected = expected + jnp.where((x == 0) & (z > 0), nx, 0)
     expected = expected + jnp.where(turns & (z == nz - 1), 1, 0)
     pl.semaphore_wait(barrier, expected)
@@ -238,19 +254,24 @@
 
     col_copies = send_peaks(0, col_group, col_peaks, col_send, col_recv)
     for m in range(3):
-        for i in range(CHUNKS):
+        for i in range(CHUNKS if m < 2 else EARLY):
             links[m][i].start()
         owns[m].start()
 
+    @pl.when(jnp.logical_not(holds))
+    def _():
+        for i in range(EARLY, CHUNKS):
+            links[2][i].start()
+
     for xx, device in zip(x_group, x_devices):
 
-        @pl.when(xx < x)
+        @pl.when(x_rank(xx, nx, x_late) < place)
         def _():
             signal(x_ack, device)
 
     for yy, device in zip(y_group, y_devices):
 
-        @pl.when(start_rank(yy, ny) < rank)
+        @pl.when(start_rank(yy, ny, y_late) < rank)
         def _():
             signal(y_ack, device)
 
@@ -278,9 +299,9 @@
 
     take_peaks(0, col_copies, col_peaks)
 
-    @pl.when(x < nx - 1)
-    def _():
-        pl.semaphore_wait(x_ack, nx - 1 - x)
+    @pl.when(place < nx - 1)
+    def _():
+        pl.semaphore_wait(x_ack, nx - 1 - place)
 
     x_copies = send_peaks(1, x_devices, x_peaks, x_send, x_recv)
     for i in range(CHUNKS):
@@ -310,65 +331,71 @@
         guess = (sides_of + product(high[0], low[0], guess)) * every
     guess_high, guess_low = split(guess)
 
-    def piece(q):
-        return pl.ds(pl.multiple_of(q * share, share), share)
-
-    def shift(source, q, device):
+    units = rows // UNIT
+    per_piece = units // (rows // share)
+
+    def unit(u):
+        return slice(u * UNIT, (u + 1) * UNIT)
+
+    def shift(u, device):
         return pltpu.make_async_remote_copy(
-            src_ref=source,
-            dst_ref=below.at[piece(q), :],
-            send_sem=shift_send.at[q],
-            recv_sem=shift_recv.at[q],
+            src_ref=solved.at[unit(u), :],
+            dst_ref=below.at[unit(u), :],
+            send_sem=shift_send.at[u],
+            recv_sem=shift_recv.at[u],
             device_id=(device, col),
             device_id_type=MESH,
         )
 
-    def forward():
+    def detour(u, target, slot):
         return pltpu.make_async_remote_copy(
-            src_ref=hop,
-            dst_ref=below.at[piece(x + 1), :],
-            send_sem=forward_send.at[0],
-            recv_sem=shift_recv.at[x + 1],
+            src_ref=solved.at[unit(u), :],
+            dst_ref=hop.at[slot],
+            send_sem=shift_send.at[u],
+            recv_sem=hop_recv.at[slot],
+            device_id=(at(y, z, target), col),
+            device_id_type=MESH,
+        )
+
+    def forward(slot, u):
+        return pltpu.make_async_remote_copy(
+            src_ref=hop.at[slot],
+            dst_ref=below.at[pl.ds(pl.multiple_of(u * UNIT, UNIT), UNIT), :],
+            send_sem=forward_send.at[slot],
+            recv_sem=shift_recv.at[u],
             device_id=(head, col),
             device_id_type=MESH,
         )
 
-    def detour(q):
-        return pltpu.make_async_remote_copy(
-            src_ref=solved.at[piece(q), :],
-            dst_ref=hop,
-            send_sem=hop_send.at[q - 1],
-            recv_sem=hop_recv.at[0],
-            device_id=(at(y, z, q - 1), col),
-            device_id_type=MESH,
-        )
-
     @pl.when(turns & (z < nz - 1))
     def _():
         pl.semaphore_wait(next_ack, 1)
 
     pieces = rows // share
-    for q in range(pieces):
+    for q in reversed(range(pieces)):
         part = slice(q * share, (q + 1) * share)
         term = dot(high[0, part, :], guess_high) + (
             dot(high[0, part, :], guess_low) + dot(low[0, part, :], guess_high)
         )
         solved[part, :] = (right[part, :] + term) * inverse[q]
 
-        if q == 0:
-
-            @pl.when(jnp.logical_not(last) | turns)
-            def _():
-                shift(solved.at[piece(0), :], 0, lvl + 1).start()
-        else:
-
-            @pl.when(jnp.logical_not(last))
-            def _():
-                shift(solved.at[piece(q), :], q, lvl + 1).start()
-
-            @pl.when(last & turns)
-            def _():
-                detour(q).start()
+        mine_of = [u for u in reversed(range(units)) if u * UNIT // share == q]
+
+        @pl.when(jnp.logical_not(last))
+        def _():
+            for u in mine_of:
+                shift(u, lvl + 1).start()
+
+        @pl.when(last & turns & (z < nz - 1))
+        def _():
+            for u in mine_of:
+                (detour(u, q - 1, u % per_piece) if q else shift(u, lvl + 1)).start()
+
+        @pl.when(last & turns & (z == nz - 1))
+        def _():
+            for u in mine_of:
+                route = LATE_ROUTES[u]
+                (shift(u, lvl + 1) if route == STRAIGHT else detour(u, route, slot_of(u))).start()
 
     take_peaks(2, y_copies, y_peaks)
 
@@ -400,12 +427,37 @@
         for copy in behind:
             copy.start()
 
-    hands_over = jnp.logical_not(last) & turns
-
-    @pl.when(hands_over)
-    def _():
-        detour(1).wait_recv()
-        forward().start()
+    def rest():
+        for i in range(EARLY, CHUNKS):
+            links[2][i].start()
+
+    @pl.when(holds & last)
+    def _():
+        rest()
+
+    def hand_over(act):
+        @pl.when((z < nz - 1) & jnp.logical_not(last))
+        def _():
+            for slot in reversed(range(per_piece)):
+                act(slot, forward(slot, per_piece * (x + 1) + slot))
+
+        for route in sorted(set(LATE_ROUTES) - {STRAIGHT}):
+
+            @pl.when((z == nz - 1) & (x == route) & turns)
+            def _():
+                for u in reversed(range(units)):
+                    if LATE_ROUTES[u] == route:
+                        act(slot_of(u), forward(slot_of(u), u))
+
+    def take_and_start(slot, copy):
+        detour(0, 0, slot).wait_recv()
+        copy.start()
+
+    hand_over(take_and_start)
+
+    @pl.when(holds & jnp.logical_not(last))
+    def _():
+        rest()
 
     for i in range(CHUNKS):
         hand_on(1, i)
@@ -425,23 +477,25 @@
     def _():
         below[...] = jnp.zeros_like(below)
 
-    lower = 0.0
-    for half in range(2):
-        part = slice(half * rows // 2, (half + 1) * rows // 2)
-
-        @pl.when(lvl > 0)
-        def _():
-            for q in range(half * pieces // 2, (half + 1) * pieces // 2):
-                shift(solved.at[piece(q), :], q, lvl).wait_recv()
-
-        lower = lower + product(high[1, :, part], low[1, :, part], below[part, :])
     best = peaks[3]
     for slot in range(3):
         z_copy(slot, z, side, 0).wait_recv()
         best = jnp.maximum(best, z_peaks[slot])
     factor = 1.0 / jnp.max(best, keepdims=True)
-    out_level[0] = (mine_even[...] + upper[:, share:] + lower[:, :share]) * factor
+    out_level[0] = (mine_even[...] + upper[:, share:]) * factor
     out_up[0] = upper[:, :share] * factor
+
+    lower = 0.0
+    for q in reversed(range(pieces)):
+        part = slice(q * share, (q + 1) * share)
+
+        @pl.when(lvl > 0)
+        def _():
+            for u in range(q * per_piece, (q + 1) * per_piece):
+                shift(u, lvl).wait_recv()
+
+        lower = lower + product(high[1, :, part], low[1, :, part], below[part, :])
+    out_level[0] = out_level[0] + lower[:, :share] * factor
     out_down[0] = lower[:, share:] * factor
 
     for copy in col_copies + x_copies + y_copies + owns:
@@ -463,21 +517,21 @@
 
     @pl.when(jnp.logical_not(last) | turns)
     def _():
-        shift(solved.at[piece(0), :], 0, lvl).wait_send()
-
-    @pl.when(jnp.logical_not(last))
-    def _():
-        for q in range(1, pieces):
-            shift(solved.at[piece(q), :], q, lvl).wait_send()
-
-    @pl.when(last & turns)
-    def _():
-        for q in range(1, pieces):
-            detour(q).wait_send()
-
-    @pl.when(hands_over)
-    def _():
-        forward().wait_send()
+        for u in range(units):
+            shift(u, lvl).wait_send()
+
+    hand_over(lambda slot, copy: copy.wait_send())
+
+
+def place_results(level, up, down, out_level, out_up, out_down, sem):
+    copies = [
+        pltpu.make_async_copy(source, target, sem.at[i])
+        for i, (source, target) in enumerate(((level, out_level), (up, out_up), (down, out_down)))
+    ]
+    for copy in copies:
+        copy.start()
+    for copy in copies:
+        copy.wait()
 
 
 def per_device(sides, up, level, down):
@@ -487,7 +541,7 @@
     regular = pltpu.SemaphoreType.REGULAR
     tile = (8, share)
     block = jax.ShapeDtypeStruct((1, rows, share), F32)
-    return pl.pallas_call(
+    results = pl.pallas_call(
         functools.partial(kernel, sides),
         out_shape=(block, block, block),
         in_specs=[pl.BlockSpec(memory_space=pl.ANY)] * 3,
@@ -501,7 +555,7 @@
             pltpu.VMEM((2, share, share), F32),
             pltpu.VMEM((rows, 2 * share), F32),
             pltpu.VMEM((rows, 2 * share), F32),
-            pltpu.VMEM((share, 2 * share), F32),
+            pltpu.VMEM((rows // UNIT // 2, UNIT, 2 * share), F32),
             pltpu.VMEM((rows, 2 * share), F32),
             pltpu.VMEM((4,) + tile, F32),
             pltpu.VMEM((3,) + tile, F32),
@@ -515,11 +569,10 @@
             dma((3, CHUNKS)),
             dma((3,)),
             dma((3,)),
-            dma((rows // share,)),
-            dma((rows // share,)),
-            dma((nx - 1,)),
-            dma((1,)),
-            dma((1,)),
+            dma((rows // UNIT,)),
+            dma((rows // UNIT,)),
+            dma((rows // UNIT // 2,)),
+            dma((rows // UNIT // 2,)),
             dma((3,)),
             dma((3,)),
             dma((nx - 1,)),
@@ -534,9 +587,17 @@
             regular,
         ],
         compiler_params=pltpu.CompilerParams(
-            collective_id=0, has_side_effects=True, vmem_limit_bytes=62 * 1024 * 1024
+            collective_id=0, has_side_effects=True, vmem_limit_bytes=40 * 1024 * 1024
         ),
-    )(up, level, down)
+    )(*(pltpu.with_memory_space_constraint(v, pltpu.HBM) for v in (up, level, down)))
+    return pl.pallas_call(
+        place_results,
+        out_shape=(block, block, block),
+        in_specs=[pl.BlockSpec(memory_space=pltpu.VMEM)] * 3,
+        out_specs=(pl.BlockSpec(memory_space=pl.ANY),) * 3,
+        scratch_shapes=[dma((3,))],
+        compiler_params=pltpu.CompilerParams(vmem_limit_bytes=8 * 1024 * 1024),
+    )(*results)
 
 
 def solution(mesh, sides=(8, 4, 4)):

time: 47.5 us -> 41.8 us (0.88)
  local copies, waits for them, and re-layouts: 3.46 us -> 0 us
  Pallas kernels: 42.8 us -> 40.6 us
    unnamed x7 -> x0, local copies, waits for them, and re-layouts: 3.46 us -> none
    pallas_call x1, Pallas kernels: 42.8 us -> 39.7 us  [per_device(): pl.pallas_call(functools.partial(kernel, sides), out_shape=(block, block,...]
    pallas_call x0 -> x1, Pallas kernels: none -> 0.9 us  [per_device(): pl.pallas_call(place_results, out_shape=(block, block, block), in_specs=[...]
where the time goes in v3:
time: 41.8 us; the launch traced here: 41.2 us
  Pallas kernels  40.6 us (97%)
  between operations  0.64 us (2%)
    pallas_call x1, Pallas kernels, per_device(): pl.pallas_call(functools.partial(kernel, sides), out_shape=(block, block,...  39.7 us
    pallas_call x1, Pallas kernels, per_device(): pl.pallas_call(place_results, out_shape=(block, block, block), in_specs=[...  0.9 us

profile of v3, /device:TPU:57, one launch (start us, length us, event | category | flops | bytes accessed | tf_op | source)
XLA Modules:
  0.0 41.2 jit_solution(3508537715467096421)
XLA Ops:
  0.6 39.7 %shard_map.58 = (f32[1,512,128]{2,1,0:T(8,128)S(1)}, f32[1,512,128]{2,1,0:T(8,128)S(1)}, f32[1,512,128]{2,1,0:T(8,128)S(1)}) custom-call(f32[2,512,128]{2,1,0:T(8,128)} %up.1, f32[2,512,128]{2,1,0:T(8,128)} %level.1, f32[2,512,128]{2,1,0:T(8,128)} %down.1), custom_call_target="tpu_custom_call" | custom-call | tf_op jit(solution)/shard_map/pallas_call | solution.py:544
  40.3 0.9 %shard_map.59 = (f32[1,512,128]{2,1,0:T(8,128)}, f32[1,512,128]{2,1,0:T(8,128)}, f32[1,512,128]{2,1,0:T(8,128)}) custom-call(f32[1,512,128]{2,1,0:T(8,128)S(1)} %get-tuple-element.6.level, f32[1,512,128]{2,1,0:T(8,128)S(1)} %get-tuple-element.7.up, f32[1,512,128]{2,1,0:T(8,128)S(1)} %get-tuple-element.8.down), custom_call_target="tpu_custom_call" | custom-call | tf_op jit(solution)/shard_map/pallas_call | solution.py:593

commit v4 on v3

--- a/solution.py
+++ b/solution.py
@@ -15,7 +15,7 @@
 EARLY = 1
 UNIT = 64
 STRAIGHT = -1
-LATE_ROUTES = (-1, -1, -1, -1, 0, 0, 2, 2)
+LATE_ROUTES = (-1, -1, -1, 0, 0, 0, 2, 2)
 
 
 def slot_of(u):
@@ -253,15 +253,10 @@
     owns = [own(m) for m in range(3)]
 
     col_copies = send_peaks(0, col_group, col_peaks, col_send, col_recv)
+    for i in range(CHUNKS):
+        links[0][i].start()
     for m in range(3):
-        for i in range(CHUNKS if m < 2 else EARLY):
-            links[m][i].start()
         owns[m].start()
-
-    @pl.when(jnp.logical_not(holds))
-    def _():
-        for i in range(EARLY, CHUNKS):
-            links[2][i].start()
 
     for xx, device in zip(x_group, x_devices):
 
@@ -304,8 +299,11 @@
         pl.semaphore_wait(x_ack, nx - 1 - place)
 
     x_copies = send_peaks(1, x_devices, x_peaks, x_send, x_recv)
+    for i in range(CHUNKS - 1):
+        hand_on(0, i)
     for i in range(CHUNKS):
-        hand_on(0, i)
+        links[1][i].start()
+    hand_on(0, CHUNKS - 1)
     take_peaks(1, x_copies, x_peaks)
 
     @pl.when(rank < ny - 1)
@@ -316,6 +314,13 @@
     gathered(0)
     local[2].wait()
     local[3].wait()
+    for i in range(EARLY):
+        links[2][i].start()
+
+    @pl.when(jnp.logical_not(holds))
+    def _():
+        for i in range(EARLY, CHUNKS):
+            links[2][i].start()
 
     inverse = []
     for s in range(rows // share):
@@ -386,16 +391,18 @@
             for u in mine_of:
                 shift(u, lvl + 1).start()
 
-        @pl.when(last & turns & (z < nz - 1))
-        def _():
-            for u in mine_of:
-                (detour(u, q - 1, u % per_piece) if q else shift(u, lvl + 1)).start()
-
-        @pl.when(last & turns & (z == nz - 1))
-        def _():
-            for u in mine_of:
-                route = LATE_ROUTES[u]
-                (shift(u, lvl + 1) if route == STRAIGHT else detour(u, route, slot_of(u))).start()
+        if q > 0:
+
+            @pl.when(last & turns & (z < nz - 1))
+            def _():
+                for u in mine_of:
+                    detour(u, q - 1, u % per_piece).start()
+
+            @pl.when(last & turns & (z == nz - 1))
+            def _():
+                for u in mine_of:
+                    route = LATE_ROUTES[u]
+                    (shift(u, lvl + 1) if route == STRAIGHT else detour(u, route, slot_of(u))).start()
 
     take_peaks(2, y_copies, y_peaks)
 
@@ -433,6 +440,8 @@
 
     @pl.when(holds & last)
     def _():
+        for u in reversed(range(per_piece)):
+            shift(u, lvl + 1).start()
         rest()
 
     def hand_over(act):
@@ -462,6 +471,12 @@
     for i in range(CHUNKS):
         hand_on(1, i)
     gathered(1)
+
+    @pl.when(last & turns & (z < nz - 1))
+    def _():
+        for u in reversed(range(per_piece)):
+            shift(u, lvl + 1).start()
+
     u_high, u_low = split(full[1])
     upper[...] = product(u_high, u_low, solved[...])
 
@@ -477,6 +492,17 @@
     def _():
         below[...] = jnp.zeros_like(below)
 
+    def lower_half(half):
+        part = slice(half * rows // 2, (half + 1) * rows // 2)
+
+        @pl.when(lvl > 0)
+        def _():
+            for u in range(half * units // 2, (half + 1) * units // 2):
+                shift(u, lvl).wait_recv()
+
+        return product(high[1, :, part], low[1, :, part], below[part, :])
+
+    lower = lower_half(1)
     best = peaks[3]
     for slot in range(3):
         z_copy(slot, z, side, 0).wait_recv()
@@ -484,17 +510,7 @@
     factor = 1.0 / jnp.max(best, keepdims=True)
     out_level[0] = (mine_even[...] + upper[:, share:]) * factor
     out_up[0] = upper[:, :share] * factor
-
-    lower = 0.0
-    for q in reversed(range(pieces)):
-        part = slice(q * share, (q + 1) * share)
-
-        @pl.when(lvl > 0)
-        def _():
-            for u in range(q * per_piece, (q + 1) * per_piece):
-                shift(u, lvl).wait_recv()
-
-        lower = lower + product(high[1, :, part], low[1, :, part], below[part, :])
+    lower = lower + lower_half(0)
     out_level[0] = out_level[0] + lower[:, :share] * factor
     out_down[0] = lower[:, share:] * factor
 

time: 41.8 us -> 40.7 us (0.974)
  the two profiles are of different devices: /device:TPU:57 before, /device:TPU:25 now
where the time goes in v4:
time: 40.7 us; the launch traced here: 40.6 us
  Pallas kernels  40 us (98%)
  between operations  0.64 us (2%)
    pallas_call x1, Pallas kernels, per_device(): pl.pallas_call(functools.partial(kernel, sides), out_shape=(block, block,...  39.1 us
    pallas_call x1, Pallas kernels, per_device(): pl.pallas_call(place_results, out_shape=(block, block, block), in_specs=[...  0.9 us

profile of v4, /device:TPU:25, one launch (start us, length us, event | category | flops | bytes accessed | tf_op | source)
XLA Modules:
  0.0 40.6 jit_solution(10244215500586153990)
XLA Ops:
  0.6 39.1 %shard_map.58 = (f32[1,512,128]{2,1,0:T(8,128)S(1)}, f32[1,512,128]{2,1,0:T(8,128)S(1)}, f32[1,512,128]{2,1,0:T(8,128)S(1)}) custom-call(f32[2,512,128]{2,1,0:T(8,128)} %up.1, f32[2,512,128]{2,1,0:T(8,128)} %level.1, f32[2,512,128]{2,1,0:T(8,128)} %down.1), custom_call_target="tpu_custom_call" | custom-call | tf_op jit(solution)/shard_map/pallas_call | solution.py:560
  39.7 0.9 %shard_map.59 = (f32[1,512,128]{2,1,0:T(8,128)}, f32[1,512,128]{2,1,0:T(8,128)}, f32[1,512,128]{2,1,0:T(8,128)}) custom-call(f32[1,512,128]{2,1,0:T(8,128)S(1)} %get-tuple-element.6.level, f32[1,512,128]{2,1,0:T(8,128)S(1)} %get-tuple-element.7.up, f32[1,512,128]{2,1,0:T(8,128)S(1)} %get-tuple-element.8.down), custom_call_target="tpu_custom_call" | custom-call | tf_op jit(solution)/shard_map/pallas_call | solution.py:609

commit v5 on v4

--- a/solution.py
+++ b/solution.py
@@ -15,7 +15,7 @@
 EARLY = 1
 UNIT = 64
 STRAIGHT = -1
-LATE_ROUTES = (-1, -1, -1, 0, 0, 0, 2, 2)
+LATE_ROUTES = (-1, -1, -1, 1, 0, 0, 2, 2)
 
 
 def slot_of(u):
@@ -38,7 +38,7 @@
 
 
 def start_rank(y, ny, first_last):
-    rank = jnp.where(y == 0, 0, jnp.where(2 * y <= ny, 2 * y - 1, 2 * (ny - y)))
+    rank = jnp.where(2 * y < ny, y, ny + ny // 2 - 1 - y)
     return jnp.where(first_last, jnp.where(y == 0, ny - 1, rank - 1), rank)
 
 
@@ -169,10 +169,6 @@
             for half in range(2):
                 signal(barrier, (at(y, zz, x), half * 2 + core))
 
-    @pl.when(turns & (z < nz - 1))
-    def _():
-        signal(barrier, (head, col))
-
     @pl.when((x == 0) & (z == 0) & (run > 0))
     def _():
         for xx in range(nx):
@@ -187,7 +183,6 @@
     peaks[0] = jnp.max(rates.reshape(share // 8, 8, share), axis=0)
 
     expected = 3 + place + rank + 2 * z
-    expected = expected + jnp.where((x == 0) & (z > 0), nx, 0)
     expected = expected + jnp.where(turns & (z == nz - 1), 1, 0)
     pl.semaphore_wait(barrier, expected)
 
@@ -279,8 +274,7 @@
 
     @pl.when((x == 0) & (z > 0))
     def _():
-        for xx in range(nx):
-            signal(next_ack, (lvl - nx + xx, col))
+        signal(next_ack, (lvl - nx, col))
 
     def hand_on(m, i):
         links[m][i].wait_recv()
@@ -299,8 +293,16 @@
         pl.semaphore_wait(x_ack, nx - 1 - place)
 
     x_copies = send_peaks(1, x_devices, x_peaks, x_send, x_recv)
-    for i in range(CHUNKS - 1):
+    for i in range(CHUNKS - 2):
         hand_on(0, i)
+
+    @pl.when((x == 0) & (z < nz - 1))
+    def _():
+        pl.semaphore_wait(next_ack, 1)
+        for xx in range(1, nx):
+            signal(next_ack, (lvl + xx, col))
+
+    hand_on(0, CHUNKS - 2)
     for i in range(CHUNKS):
         links[1][i].start()
     hand_on(0, CHUNKS - 1)
@@ -372,7 +374,7 @@
             device_id_type=MESH,
         )
 
-    @pl.when(turns & (z < nz - 1))
+    @pl.when((x > 0) & (z < nz - 1))
     def _():
         pl.semaphore_wait(next_ack, 1)
 
@@ -398,11 +400,11 @@
                 for u in mine_of:
                     detour(u, q - 1, u % per_piece).start()
 
-            @pl.when(last & turns & (z == nz - 1))
-            def _():
-                for u in mine_of:
-                    route = LATE_ROUTES[u]
-                    (shift(u, lvl + 1) if route == STRAIGHT else detour(u, route, slot_of(u))).start()
+        @pl.when(last & turns & (z == nz - 1))
+        def _():
+            for u in mine_of:
+                route = LATE_ROUTES[u]
+                (shift(u, lvl + 1) if route == STRAIGHT else detour(u, route, slot_of(u))).start()
 
     take_peaks(2, y_copies, y_peaks)
 
@@ -440,8 +442,6 @@
 
     @pl.when(holds & last)
     def _():
-        for u in reversed(range(per_piece)):
-            shift(u, lvl + 1).start()
         rest()
 
     def hand_over(act):

time: 40.7 us -> 40 us (0.983)
  the two profiles are of different devices: /device:TPU:25 before, /device:TPU:57 now
where the time goes in v5:
time: 40 us; the launch traced here: 39.9 us
  Pallas kernels  39.3 us (98%)
  between operations  0.64 us (2%)
    pallas_call x1, Pallas kernels, per_device(): pl.pallas_call(functools.partial(kernel, sides), out_shape=(block, block,...  38.4 us
    pallas_call x1, Pallas kernels, per_device(): pl.pallas_call(place_results, out_shape=(block, block, block), in_specs=[...  0.9 us

profile of v5, /device:TPU:57, one launch (start us, length us, event | category | flops | bytes accessed | tf_op | source)
XLA Modules:
  0.0 39.9 jit_solution(16364777123221130513)
XLA Ops:
  0.6 38.4 %shard_map.58 = (f32[1,512,128]{2,1,0:T(8,128)S(1)}, f32[1,512,128]{2,1,0:T(8,128)S(1)}, f32[1,512,128]{2,1,0:T(8,128)S(1)}) custom-call(f32[2,512,128]{2,1,0:T(8,128)} %up.1, f32[2,512,128]{2,1,0:T(8,128)} %level.1, f32[2,512,128]{2,1,0:T(8,128)} %down.1), custom_call_target="tpu_custom_call" | custom-call | tf_op jit(solution)/shard_map/pallas_call | solution.py:560
  39.0 0.9 %shard_map.59 = (f32[1,512,128]{2,1,0:T(8,128)}, f32[1,512,128]{2,1,0:T(8,128)}, f32[1,512,128]{2,1,0:T(8,128)}) custom-call(f32[1,512,128]{2,1,0:T(8,128)S(1)} %get-tuple-element.6.level, f32[1,512,128]{2,1,0:T(8,128)S(1)} %get-tuple-element.7.up, f32[1,512,128]{2,1,0:T(8,128)S(1)} %get-tuple-element.8.down), custom_call_target="tpu_custom_call" | custom-call | tf_op jit(solution)/shard_map/pallas_call | solution.py:609

commit v6 on v5

--- a/solution.py
+++ b/solution.py
@@ -11,8 +11,8 @@
 MESH = pl.DeviceIdType.MESH
 F32 = jnp.float32
 BF16 = jnp.bfloat16
-CHUNKS = 4
-EARLY = 1
+CHUNKS = 8
+EARLY = 2
 UNIT = 64
 STRAIGHT = -1
 LATE_ROUTES = (-1, -1, -1, 1, 0, 0, 2, 2)

time: 40 us -> 39.9 us (level)
  no operation moved by 1% of the time
where the time goes in v6:
time: 39.9 us; the launch traced here: 39.7 us
  Pallas kernels  39.1 us (98%)
  between operations  0.64 us (2%)
    pallas_call x1, Pallas kernels, per_device(): pl.pallas_call(functools.partial(kernel, sides), out_shape=(block, block,...  38.2 us
    pallas_call x1, Pallas kernels, per_device(): pl.pallas_call(place_results, out_shape=(block, block, block), in_specs=[...  0.9 us

profile of v6, /device:TPU:57, one launch (start us, length us, event | category | flops | bytes accessed | tf_op | source)
XLA Modules:
  0.0 39.7 jit_solution(14057175634124290832)
XLA Ops:
  0.6 38.2 %shard_map.58 = (f32[1,512,128]{2,1,0:T(8,128)S(1)}, f32[1,512,128]{2,1,0:T(8,128)S(1)}, f32[1,512,128]{2,1,0:T(8,128)S(1)}) custom-call(f32[2,512,128]{2,1,0:T(8,128)} %up.1, f32[2,512,128]{2,1,0:T(8,128)} %level.1, f32[2,512,128]{2,1,0:T(8,128)} %down.1), custom_call_target="tpu_custom_call" | custom-call | tf_op jit(solution)/shard_map/pallas_call | solution.py:560
  38.8 0.9 %shard_map.59 = (f32[1,512,128]{2,1,0:T(8,128)}, f32[1,512,128]{2,1,0:T(8,128)}, f32[1,512,128]{2,1,0:T(8,128)}) custom-call(f32[1,512,128]{2,1,0:T(8,128)S(1)} %get-tuple-element.6.level, f32[1,512,128]{2,1,0:T(8,128)S(1)} %get-tuple-element.7.up, f32[1,512,128]{2,1,0:T(8,128)S(1)} %get-tuple-element.8.down), custom_call_target="tpu_custom_call" | custom-call | tf_op jit(solution)/shard_map/pallas_call | solution.py:609
